TPU v7x, 32 devices: a whole 2x2x4 slice. The times are simulated.
32 devices in a mesh: doc: 4 (over z), feat: 8 (over y, x, core).
Axes of the slice: x: 2, y: 2, z: 4, core: 2. Of those that a mesh axis runs over, the one named last changes fastest.
Arguments:
- documents: bfloat16 [512, 512], P('doc', 'feat'), may hold values from -6 to 6
- directions: bfloat16 [512, 32768], P('doc', 'feat'), may hold values from -0.5 to 0.5
- phase: float32 [32768], P('feat'), may hold values from -3.140625 to 3.140625
- amplitude: float32 [32768], P('feat'), may hold values from 0.4 to 2.3
- doc_weight: float32 [512], P('doc'), may hold values from 0.5 to 4.2
- labels: int32 [512], P('doc'), may hold values from 0 to 127
Outputs:
- margins: float32 [512, 128], P('doc')
- scaled_weights: float32 [32768, 128], P('feat')
All inputs are finite; a program needn't handle non-finite values.
Results may differ from a plain program's by a relative error of at most 0.0003.
Values may be sent and summed in bfloat16 or wider, within the bound.
A program may use at most 64 MiB of HBM per device.

v0:
```python
import jax
import jax.numpy as jnp
from jax import lax
from jax.sharding import PartitionSpec as P

C = 128
ITERS = 3
NEWTON = 3
HI = lax.Precision.HIGHEST
shrink_level = 0.1
ratio_floor = 1e-06


def logistic_prox(target, signs, weight_ratio):
    current = target
    for newton_step in range(NEWTON):
        chance = jax.nn.sigmoid(-signs * current)
        gradient = current - target - weight_ratio * signs * chance
        current = current - gradient / (1.0 + weight_ratio * chance * (1.0 - chance))
    return current


def shrink_values(target, limit):
    return target - jnp.clip(target, -limit, limit)


def per_device(documents, directions, phase, amplitude, doc_weight, labels):
    doc_count = documents.shape[0]
    width_tile = directions.shape[1]
    num_feat = lax.axis_size("feat")
    num_doc = lax.axis_size("doc")
    chunk = width_tile // num_doc
    row = lax.axis_index("doc")
    doc_rows = lax.all_gather(documents, "feat", axis=1, tiled=True)
    doc_full = lax.all_gather(doc_rows, "doc", axis=0, tiled=True)
    dir_chunk = lax.all_to_all(directions, "doc", split_axis=1, concat_axis=0, tiled=True)
    phase_c = lax.dynamic_slice_in_dim(phase, row * chunk, chunk, 0)
    amp_c = lax.dynamic_slice_in_dim(amplitude, row * chunk, chunk, 0)
    angles = jnp.dot(doc_full, dir_chunk, preferred_element_type=jnp.float32)
    features = jnp.sqrt(2.0 / width_tile) * amp_c * jnp.cos(angles + phase_c)
    blocks = features.reshape(num_doc, doc_count, chunk)
    gram = jnp.einsum("iac,ibc->iab", blocks, blocks, precision=HI)
    gram = lax.psum_scatter(gram, "doc", scatter_dimension=0, tiled=True)[0]
    eye = jnp.eye(doc_count, dtype=jnp.float32)
    factor = jnp.linalg.cholesky(eye + gram)
    lower_inv = lax.linalg.triangular_solve(factor, eye, left_side=True, lower=True)
    inverse = lax.dot_general(lower_inv, lower_inv, (((0,), (0,)), ((), ())), precision=HI)
    signs = jnp.where(labels[:, None] == jnp.arange(C, dtype=jnp.int32)[None, :], 1.0, -1.0).astype(
        jnp.float32
    )
    share_rows = doc_count // num_feat
    offset = lax.axis_index("feat") * share_rows
    signs = lax.dynamic_slice_in_dim(signs, offset, share_rows, 0)
    weight = lax.dynamic_slice_in_dim(doc_weight, offset, share_rows, 0)[:, None]
    rho = jnp.float32(1.0)
    margins = logistic_prox(jnp.zeros(signs.shape, jnp.float32), signs, weight / rho)
    sums = jnp.zeros(signs.shape, jnp.float32)
    duals_y = jnp.zeros(signs.shape, jnp.float32)
    part = jnp.zeros((doc_count, C), jnp.float32)
    image = jnp.zeros((doc_count, C), jnp.float32)
    weights = jnp.zeros((chunk, C), jnp.float32)
    product = jnp.zeros((doc_count, C), jnp.float32)
    for step in range(ITERS):
        correction = (margins - duals_y - sums) / num_feat
        correction = lax.all_gather(correction, "feat", axis=0, tiled=True)
        target = part + correction
        residue = target - image
        solved = jnp.dot(inverse, residue, precision=HI)
        applied = residue - solved
        part = target - solved
        sums = lax.psum_scatter(part, "feat", scatter_dimension=0, tiled=True)
        all_solved = lax.all_gather(solved, "doc", axis=0, tiled=True)
        lifted = lax.dot_general(features, all_solved, (((0,), (0,)), ((), ())), precision=HI)
        old_weights = weights
        old_margins = margins
        weights = shrink_values(weights + lifted / num_doc, shrink_level / (rho * num_doc))
        margins = logistic_prox(sums + duals_y, signs, weight / rho)
        duals_y = duals_y + sums - margins
        if step + 1 < ITERS:
            move = old_weights - weights
            if step == 0:
                d_move, d_solved, d_applied, d_lifted = (move, solved, applied, lifted)
            else:
                d_move = move - last_move / growth
                d_solved = solved - last_solved / growth
                d_applied = applied - last_applied / growth
                d_lifted = lifted - last_lifted / growth
            primal = (
                jnp.sum(num_doc * d_move * d_move + 2.0 * d_move * d_lifted)
                + jnp.sum(d_solved * d_applied)
                + jnp.sum((sums - margins) ** 2)
            )
            dual = num_doc * jnp.sum(move**2) + jnp.sum((margins - old_margins) ** 2)
            primal, dual = lax.psum((primal, dual), ("doc", "feat"))
            primal = jnp.maximum(primal, 0.0)
            new_product = jnp.dot(features, weights, precision=HI)
            new_product = lax.psum_scatter(new_product, "doc", scatter_dimension=0, tiled=True)
            growth = ((primal + ratio_floor) / (rho * rho * dual + ratio_floor)) ** 0.25
            rho = rho * growth
            duals_y = duals_y / growth
            image = new_product - (product - new_product + applied) / growth
            product = new_product
            last_move, last_solved, last_applied, last_lifted = (move, solved, applied, lifted)
    margins = lax.all_gather(margins, "feat", axis=0, tiled=True)
    weights = lax.all_gather(num_feat * weights, "doc", axis=0, tiled=True)
    return (margins, weights)


def solution(mesh):
    in_specs = (P("doc", "feat"), P("doc", "feat"), P("feat"), P("feat"), P("doc"), P("doc"))
    out_specs = (P("doc", None), P("feat", None))
    return jax.shard_map(
        per_device, mesh=mesh, in_specs=in_specs, out_specs=out_specs, check_vma=False
    )
```

profile of v0, /device:TPU:0, one launch (start us, length us, event | category | flops | bytes accessed | tf_op | source)
XLA Modules:
  0.0 383.9 jit_solution(2985545460666034803)
XLA Ops:
  7.2 2.3 copy.10
  9.4 6.3 %all-to-all-start = ((bf16[128,4,1024]{0,2,1:T(8,128)(2,1)}), bf16[128,4,1024]{0,2,1:T(8,128)(2,1)S(1)}, u32[]{:S(2)}, u32[]{:S(2)}) async-start(bf16[128,4,1024]{0,2,1:T(8,128)(2,1)} %bitcast), calls=%async_computation | async-start | bytes 2097152 | tf_op jit(solution)/shard_map/all_to_all | solution.py:36
  15.8 9.2 %all_gather.31 = bf16[128,512]{0,1:T(8,128)(2,1)S(1)} all-gather(bf16[128,64]{0,1:T(8,128)(2,1)S(1)} %copy-done.4), channel_id=1, replica_groups=mesh['doc'=4,'feat'=8] {'feat'}, dimensions={1}, use_global_device_ids=true | all-gather | bytes 147456 | tf_op jit(solution)/shard_map/all_gather | solution.py:34
  25.7 25.3 %all_gather.32 = bf16[512,512]{0,1:T(8,128)(2,1)} all-gather(bf16[128,512]{0,1:T(8,128)(2,1)S(1)} %all_gather.31), channel_id=1, replica_groups=mesh['doc'=4,'feat'=8] {'doc'}, dimensions={0}, use_global_device_ids=true | all-gather | bytes 655360 | tf_op jit(solution)/shard_map/all_gather | solution.py:35
  51.6 8.3 %cosine_multiply_fusion = f32[512,1024]{1,0:T(8,128)S(1)} fusion(bf16[512,512]{0,1:T(8,128)(2,1)} %all_gather.32, bf16[512,1024]{1,0:T(8,128)(2,1)S(1)} %bitcast.38, f32[1024]{0:T(1024)S(1)} %dynamic-slice-done, f32[1024]{0:T(1024)S(1)} %dynamic-slice_multiply_fusion), kind=kOutput, calls=%fused_computation | convolution fusion | flops 537919488 | bytes 3678208 | tf_op jit(solution)/shard_map/dot_general | solution.py:39
  59.9 2.8 fusion.142
  63.1 9.4 %all_gather.30 = f32[128,128]{1,0:T(8,128)S(1)} all-gather(f32[16,128]{1,0:T(8,128)S(1)} %broadcast_multiply_fusion), channel_id=1, replica_groups=mesh['doc'=4,'feat'=8] {'feat'}, dimensions={0}, use_global_device_ids=true | all-gather | bytes 73728 | tf_op jit(solution)/shard_map/all_gather | solution.py:65
  72.5 14.2 %reduce-scatter.7.cloned.1.call-done = f32[1,128,128]{2,1,0:T(8,128)} async-done(((f32[4,128,128]{2,1,0:T(8,128)}), f32[1,128,128]{2,1,0:T(8,128)}) %reduce-scatter.7.cloned.1.call-update) | async-done | bytes 65552 | tf_op jit(solution)/shard_map/reduce_scatter | solution.py:43
  88.5 11.7 %cholesky.18 = f32[128,128]{1,0:T(8,128)S(1)} custom-call(f32[128,128]{1,0:T(8,128)S(1)} %fusion.13), custom_call_target="Cholesky" | custom-call | tf_op jit(solution)/shard_map/jit(cholesky)/cholesky | solution.py:45
  101.6 9.8 %custom-call.6 = f32[1,128,128]{1,2,0:T(8,128)S(1)} custom-call(f32[1,128,128]{2,1,0:T(8,128)S(1)} %fusion.10), custom_call_target="InvertDiagBlocksLowerTriangular" | custom-call | tf_op jit(solution)/shard_map/triangular_solve | solution.py:46
  111.9 1.5 multiply_reduce_fusion.3
  113.5 14.1 %all_gather.33 = f32[512,128]{1,0:T(8,128)S(1)} all-gather(f32[128,128]{1,0:T(8,128)S(1)} %get-tuple-element.23), channel_id=1, replica_groups=mesh['doc'=4,'feat'=8] {'doc'}, dimensions={0}, use_global_device_ids=true | all-gather | bytes 327680 | tf_op jit(solution)/shard_map/all_gather | solution.py:72
  127.6 4.1 %multiply_reduce_fusion.1 = (f32[]{:T(128)}, f32[]{:T(128)}, f32[1024,128]{1,0:T(8,128)S(1)}) fusion(f32[512,1024]{1,0:T(8,128)S(1)} %cosine_multiply_fusion, f32[512,128]{1,0:T(8,128)S(1)} %all_gather.33), kind=kOutput, calls=%fused_computation.13 | convolution fusion | flops 806879232 | bytes 2883592 | tf_op jit(solution)/shard_map/dot_general | solution.py:73
  131.7 2.5 fusion.6
  136.2 9.2 %reduce-scatter.9.cloned.1.call-done = f32[16,128]{1,0:T(8,128)} async-done(((f32[128,128]{1,0:T(8,128)}), f32[16,128]{1,0:T(8,128)}) %reduce-scatter.9.cloned.1.call-update) | async-done | bytes 8208 | tf_op jit(solution)/shard_map/reduce_scatter | solution.py:71
  149.3 39.3 %all-reduce.1 = (f32[]{:T(128)}, f32[]{:T(128)}) all-reduce(f32[]{:T(128)S(6)} %add.203, f32[]{:T(128)S(6)} %add.205), channel_id=1, replica_groups=mesh['doc'=4,'feat'=8] {'doc','feat'}, use_global_device_ids=true, to_apply=%region_7.8 | all-reduce | flops 2 | bytes 16 | tf_op jit(solution)/shard_map/psum | solution.py:94
  190.6 10.2 %all_gather.34 = f32[128,128]{1,0:T(8,128)S(1)} all-gather(f32[16,128]{1,0:T(8,128)S(1)} %subtract_multiply_fusion.2), channel_id=1, replica_groups=mesh['doc'=4,'feat'=8] {'feat'}, dimensions={0}, use_global_device_ids=true | all-gather | bytes 73728 | tf_op jit(solution)/shard_map/all_gather | solution.py:65
  201.7 1.5 multiply_reduce_fusion.2
  203.2 14.2 %all_gather.35 = f32[512,128]{1,0:T(8,128)S(1)} all-gather(f32[128,128]{1,0:T(8,128)S(1)} %get-tuple-element.25), channel_id=1, replica_groups=mesh['doc'=4,'feat'=8] {'doc'}, dimensions={0}, use_global_device_ids=true | all-gather | bytes 327680 | tf_op jit(solution)/shard_map/all_gather | solution.py:72
  217.4 4.2 %multiply_reduce_fusion = (f32[]{:T(128)}, f32[]{:T(128)}, f32[1024,128]{1,0:T(8,128)S(1)}) fusion(f32[1024,128]{1,0:T(8,128)S(1)} %get-tuple-element.24, f32[]{:T(128)S(6)} %neg.66, f32[]{:T(128)S(6)} %div.199, f32[]{:T(128)S(6)} %pow.6, f32[512,1024]{1,0:T(8,128)S(1)} %cosine_multiply_fusion, f32[512,128]{1,0:T(8,128)S(1)} %all_gather.35), kind=kOutput, calls=%fused_computation.11 | convolution fusion | flops 808189952 | bytes 3407892 | tf_op jit(solution)/shard_map/dot_general | solution.py:73
  221.6 2.5 fusion.137
  226.1 9.7 %reduce-scatter.13.cloned.1.call-done = f32[16,128]{1,0:T(8,128)} async-done(((f32[128,128]{1,0:T(8,128)}), f32[16,128]{1,0:T(8,128)}) %reduce-scatter.13.cloned.1.call-update) | async-done | bytes 8208 | tf_op jit(solution)/shard_map/reduce_scatter | solution.py:71
  235.9 1.5 multiply_reduce_fusion.4
  238.5 39.4 %all-reduce = (f32[]{:T(128)}, f32[]{:T(128)}) all-reduce(f32[]{:T(128)S(6)} %add.219, f32[]{:T(128)S(6)} %add.221), channel_id=1, replica_groups=mesh['doc'=4,'feat'=8] {'doc','feat'}, use_global_device_ids=true, to_apply=%region_16.17 | all-reduce | flops 2 | bytes 16 | tf_op jit(solution)/shard_map/psum | solution.py:94
  279.9 11.2 %all_gather.36 = f32[128,128]{1,0:T(8,128)} all-gather(f32[16,128]{1,0:T(8,128)S(1)} %subtract_multiply_fusion.1), channel_id=1, replica_groups=mesh['doc'=4,'feat'=8] {'feat'}, dimensions={0}, use_global_device_ids=true | all-gather | bytes 73728 | tf_op jit(solution)/shard_map/all_gather | solution.py:65
  291.1 1.8 fusion.140
  292.9 14.0 %all_gather.38 = f32[512,128]{1,0:T(8,128)S(1)} all-gather(f32[128,128]{1,0:T(8,128)S(1)} %get-tuple-element.28), channel_id=1, replica_groups=mesh['doc'=4,'feat'=8] {'doc'}, dimensions={0}, use_global_device_ids=true | all-gather | bytes 327680 | tf_op jit(solution)/shard_map/all_gather | solution.py:72
  306.9 4.2 %subtract_multiply_fusion = f32[1024,128]{1,0:T(8,128)} fusion(f32[512,1024]{1,0:T(8,128)S(1)} %cosine_multiply_fusion, f32[512,128]{1,0:T(8,128)S(1)} %all_gather.38, f32[]{:T(128)S(6)} %neg.70, f32[]{:T(128)S(6)} %div.220, f32[]{:T(128)S(6)} %neg.66, f32[]{:T(128)S(6)} %div.199, f32[1024,128]{1,0:T(8,128)S(1)} %get-tuple-element.26, ...), kind=kOutput, calls=%fused_computation.10 | convolution fusion | flops 807141376 | bytes 3932176 | tf_op jit(solution)/shard_map/dot_general | solution.py:73
  311.2 14.3 %reduce-scatter.17.cloned.1.call-done = f32[16,128]{1,0:T(8,128)} async-done(((f32[128,128]{1,0:T(8,128)}), f32[16,128]{1,0:T(8,128)}) %reduce-scatter.17.cloned.1.call-update) | async-done | bytes 8208 | tf_op jit(solution)/shard_map/reduce_scatter | solution.py:71
  326.4 9.2 %all_gather.37 = f32[128,128]{1,0:T(8,128)S(1)} all-gather(f32[16,128]{1,0:T(8,128)S(1)} %fusion.63), channel_id=1, replica_groups=mesh['doc'=4,'feat'=8] {'feat'}, dimensions={0}, use_global_device_ids=true | all-gather | bytes 73728 | tf_op jit(solution)/shard_map/all_gather | solution.py:104
  335.6 37.8 %all-gather.2.cloned.1.call-done = f32[4096,128]{1,0:T(8,128)} async-done(((f32[1024,128]{1,0:T(8,128)}), f32[4096,128]{1,0:T(8,128)}) %all-gather.2.cloned.1.call-update) | async-done | bytes 2097168 | tf_op jit(solution)/shard_map/all_gather | solution.py:105
  374.0 3.0 copy.16
  (61 shorter events, 12.3 us)
Async XLA Ops:
  7.2 8.6 %copy-start.4 = (bf16[128,64]{0,1:T(8,128)(2,1)S(1)}, bf16[128,64]{0,1:T(8,128)(2,1)}, u32[]{:S(2)}) copy-start(bf16[128,64]{0,1:T(8,128)(2,1)} %param.6) | copy-start | bytes 49156
  9.4 41.6 %all-to-all-start = ((bf16[128,4,1024]{0,2,1:T(8,128)(2,1)}), bf16[128,4,1024]{0,2,1:T(8,128)(2,1)S(1)}, u32[]{:S(2)}, u32[]{:S(2)}) async-start(bf16[128,4,1024]{0,2,1:T(8,128)(2,1)} %bitcast), calls=%async_computation | async-start | bytes 2097152 | tf_op jit(solution)/shard_map/all_to_all | solution.py:36
  15.8 70.9 %reduce-scatter.7.cloned.1.call-start = ((), (), s32[]{:S(2)}) async-start(), calls=%async_computation.7 | async-start | bytes 327680 | tf_op jit(solution)/shard_map/reduce_scatter | solution.py:43
  15.8 35.8 %dynamic-slice-start = ((f32[4096]{0:T(1024)}, s32[]{:T(128)}), f32[1024]{0:T(1024)S(1)}, s32[]{:S(2)}) async-start(f32[4096]{0:T(1024)} %param.8, s32[]{:T(128)} %select_n.18), calls=%async_computation.14 | async-start | bytes 8704 | tf_op jit(solution)/shard_map/dynamic_slice | solution.py:37
  59.9 2.9 copy-start.9
  59.9 2.9 copy-start.7
  62.7 82.6 %reduce-scatter.9.cloned.1.call-start = ((), (), s32[]{:S(2)}) async-start(), calls=%async_computation.8 | async-start | bytes 73728 | tf_op jit(solution)/shard_map/reduce_scatter | solution.py:71
  62.9 173.0 %copy-start.5 = (s32[16]{0:T(128)}, s32[16]{0:T(128)S(1)}, u32[]{:S(2)}) copy-start(s32[16]{0:T(128)S(1)} %dynamic-slice) | copy-start | bytes 196
  113.5 87.4 %reduce-scatter.11.cloned.1.call-start = ((), (), s32[]{:S(2)}) async-start(), calls=%async_computation.9 | async-start | bytes 327680 | tf_op jit(solution)/shard_map/reduce_scatter | solution.py:97
  131.7 69.2 %copy-start = (f32[128,128]{1,0:T(8,128)S(1)}, f32[128,128]{1,0:T(8,128)}, u32[]{:S(2)}) copy-start(f32[128,128]{1,0:T(8,128)} %get-tuple-element.20) | copy-start | bytes 196612
  136.1 99.8 %reduce-scatter.13.cloned.1.call-start = ((), (), s32[]{:S(2)}) async-start(), calls=%async_computation.10 | async-start | bytes 73728 | tf_op jit(solution)/shard_map/reduce_scatter | solution.py:71
  203.2 87.9 %reduce-scatter.15.cloned.1.call-start = ((), (), s32[]{:S(2)}) async-start(), calls=%async_computation.11 | async-start | bytes 327680 | tf_op jit(solution)/shard_map/reduce_scatter | solution.py:97
  221.6 69.5 %copy-start.1 = (f32[128,128]{1,0:T(8,128)S(1)}, f32[128,128]{1,0:T(8,128)}, u32[]{:S(2)}) copy-start(f32[128,128]{1,0:T(8,128)} %reduce-scatter.11.cloned.1.call-done) | copy-start | bytes 196612
  221.6 69.5 %copy-start.2 = (f32[128,128]{1,0:T(8,128)S(1)}, f32[128,128]{1,0:T(8,128)}, u32[]{:S(2)}) copy-start(f32[128,128]{1,0:T(8,128)} %get-tuple-element.22) | copy-start | bytes 196612
  224.2 101.4 %reduce-scatter.17.cloned.1.call-start = ((), (), s32[]{:S(2)}) async-start(), calls=%async_computation.12 | async-start | bytes 73728 | tf_op jit(solution)/shard_map/reduce_scatter | solution.py:71
  292.9 80.5 %all-gather.2.cloned.1.call-start = ((), (), s32[]{:S(2)}) async-start(), calls=%async_computation.13 | async-start | bytes 2621440 | tf_op jit(solution)/shard_map/all_gather | solution.py:105
  306.9 4.3 %copy-start.8 = (f32[128]{0:T(128)S(1)}, f32[128]{0:T(128)}, u32[]{:S(2)}) copy-start(f32[128]{0:T(128)} %param.10) | copy-start | bytes 1540
  306.9 18.7 %copy-start.3 = (f32[16,128]{1,0:T(8,128)S(1)}, f32[16,128]{1,0:T(8,128)}, u32[]{:S(2)}) copy-start(f32[16,128]{1,0:T(8,128)} %reduce-scatter.13.cloned.1.call-done) | copy-start | bytes 24580
  306.9 18.7 %copy-start.6 = (s32[16]{0:T(128)S(1)}, s32[16]{0:T(128)}, u32[]{:S(2)}) copy-start(s32[16]{0:T(128)} %copy-done.5) | copy-start | bytes 196
Sparse Core Ops, SparseCore 0:
  62.8 23.8 reduce-scatter.6
  113.6 31.7 reduce-scatter.8
  148.2 19.9 reduce-scatter.10
  203.3 32.4 reduce-scatter.12
  238.5 19.9 reduce-scatter.14
  293.0 32.5 reduce-scatter.16
  327.7 45.6 all-gather.1
where the time goes:
time: 385 us; the launch traced here: 384 us
  blocking collectives  195 us (51%)
  waiting for transfers between devices  85.3 us (22%)
  matrix products  33.9 us (9%)
  other arithmetic  32.9 us (9%)
  between operations  23 us (6%)
  local copies, waits for them, and re-layouts  6.75 us (2%)
  starting transfers between devices  6.6 us (2%)
    psum x2, blocking collectives, per_device(): primal, dual = lax.psum((primal, dual), ('doc', 'feat'))  78.7 us
    all_gather x3, blocking collectives, per_device(): all_solved = lax.all_gather(solved, 'doc', axis=0, tiled=True)  42.2 us
    all_gather x1, waiting for transfers between devices, per_device(): weights = lax.all_gather(num_feat * weights, 'doc', axis=0, tiled=True)  37.8 us
    reduce_scatter x3, waiting for transfers between devices, per_device(): sums = lax.psum_scatter(part, 'feat', scatter_dimension=0, tiled=True)  33.2 us
    all_gather x3, blocking collectives, per_device(): correction = lax.all_gather(correction, 'feat', axis=0, tiled=True)  30.8 us
    all_gather x1, blocking collectives, per_device(): doc_full = lax.all_gather(doc_rows, 'doc', axis=0, tiled=True)  25.3 us
    reduce_scatter x1, waiting for transfers between devices, per_device(): gram = lax.psum_scatter(gram, 'doc', scatter_dimension=0, tiled=True)[0]  14.2 us
    dot_general x3, matrix products, per_device(): lax.dot_general(features, all_solved, (((0,), (0,)), ((), ())), precision...  12.5 us
  transfers between devices with their start and end apart: 8, of which 5 were waited for; matrix products, arithmetic and copies ran while one was open for 7% of the time, Pallas kernels for 0%

commit v1 on v0

--- a/solution.py
+++ b/solution.py
@@ -69,7 +69,15 @@
         applied = residue - solved
         part = target - solved
         sums = lax.psum_scatter(part, "feat", scatter_dimension=0, tiled=True)
-        all_solved = lax.all_gather(solved, "doc", axis=0, tiled=True)
+        ways, here = (lax.axis_size("doc"), lax.axis_index("doc"))
+        grown, reach = (solved, 1)
+        while reach < ways:
+            theirs = lax.ppermute(grown, "doc", [(d, d ^ reach) for d in range(ways)])
+            mine_first = jnp.concatenate([grown, theirs], axis=0)
+            theirs_first = jnp.concatenate([theirs, grown], axis=0)
+            grown = jnp.where(here & reach == 0, mine_first, theirs_first)
+            reach = 2 * reach
+        all_solved = grown
         lifted = lax.dot_general(features, all_solved, (((0,), (0,)), ((), ())), precision=HI)
         old_weights = weights
         old_margins = margins

time: 385 us -> 406 us (1.055)
  waiting for transfers between devices: 85.3 us -> 140 us
  blocking collectives: 195 us -> 152 us
  starting transfers between devices: 6.6 us -> 15.8 us
    all_gather x3 -> x0, blocking collectives: 42.2 us -> none  [per_device(): all_solved = lax.all_gather(solved, 'doc', axis=0, tiled=True)]
    ppermute x0 -> x6, waiting for transfers between devices: none -> 28.2 us  [per_device(): theirs = lax.ppermute(grown, 'doc', [(d, d ^ reach) for d in range(ways)])]
    reduce_scatter x3, waiting for transfers between devices: 33.2 us -> 59.4 us  [per_device(): sums = lax.psum_scatter(part, 'feat', scatter_dimension=0, tiled=True)]
    ppermute x0 -> x6, starting transfers between devices: none -> 8.7 us  [per_device(): theirs = lax.ppermute(grown, 'doc', [(d, d ^ reach) for d in range(ways)])]
  transfers between devices with their start and end apart: 8 -> 14, of which waited for: 5 -> 11; matrix products, arithmetic and copies ran while one was open for 7% -> 6% of each run, Pallas kernels for 0% -> 0%
where the time goes in v1:
time: 406 us; the launch traced here: 405 us
  blocking collectives  152 us (37%)
  waiting for transfers between devices  140 us (34%)
  matrix products  34.7 us (9%)
  other arithmetic  33 us (8%)
  between operations  23.2 us (6%)
  starting transfers between devices  15.8 us (4%)
  local copies, waits for them, and re-layouts  6.76 us (2%)
    psum x2, blocking collectives, per_device(): primal, dual = lax.psum((primal, dual), ('doc', 'feat'))  78.6 us
    reduce_scatter x3, waiting for transfers between devices, per_device(): sums = lax.psum_scatter(part, 'feat', scatter_dimension=0, tiled=True)  59.4 us
    all_gather x1, waiting for transfers between devices, per_device(): weights = lax.all_gather(num_feat * weights, 'doc', axis=0, tiled=True)  37.8 us
    all_gather x3, blocking collectives, per_device(): correction = lax.all_gather(correction, 'feat', axis=0, tiled=True)  29.9 us
    ppermute x6, waiting for transfers between devices, per_device(): theirs = lax.ppermute(grown, 'doc', [(d, d ^ reach) for d in range(ways)])  28.2 us
    all_gather x1, blocking collectives, per_device(): doc_full = lax.all_gather(doc_rows, 'doc', axis=0, tiled=True)  25.3 us
    reduce_scatter x1, waiting for transfers between devices, per_device(): gram = lax.psum_scatter(gram, 'doc', scatter_dimension=0, tiled=True)[0]  14.2 us
    dot_general x3, matrix products, per_device(): lax.dot_general(features, all_solved, (((0,), (0,)), ((), ())), precision...  13.5 us
  transfers between devices with their start and end apart: 14, of which 11 were waited for; matrix products, arithmetic and copies ran while one was open for 6% of the time, Pallas kernels for 0%

profile of v1, /device:TPU:0, one launch (start us, length us, event | category | flops | bytes accessed | tf_op | source)
XLA Modules:
  0.0 405.3 jit_solution(5055399684375657936)
XLA Ops:
  9.4 6.3 %all-to-all-start = ((bf16[128,4,1024]{0,2,1:T(8,128)(2,1)}), bf16[128,4,1024]{0,2,1:T(8,128)(2,1)S(1)}, u32[]{:S(2)}, u32[]{:S(2)}) async-start(bf16[128,4,1024]{0,2,1:T(8,128)(2,1)} %bitcast), calls=%async_computation | async-start | bytes 2097152 | tf_op jit(solution)/shard_map/all_to_all | solution.py:36
  15.8 9.2 %all_gather.22 = bf16[128,512]{0,1:T(8,128)(2,1)S(1)} all-gather(bf16[128,64]{0,1:T(8,128)(2,1)S(1)} %copy-done.6), channel_id=1, replica_groups=mesh['doc'=4,'feat'=8] {'feat'}, dimensions={1}, use_global_device_ids=true | all-gather | bytes 147456 | tf_op jit(solution)/shard_map/all_gather | solution.py:34
  25.7 25.3 %all_gather.23 = bf16[512,512]{0,1:T(8,128)(2,1)} all-gather(bf16[128,512]{0,1:T(8,128)(2,1)S(1)} %all_gather.22), channel_id=1, replica_groups=mesh['doc'=4,'feat'=8] {'doc'}, dimensions={0}, use_global_device_ids=true | all-gather | bytes 655360 | tf_op jit(solution)/shard_map/all_gather | solution.py:35
  51.6 8.3 %cosine_multiply_fusion = f32[512,1024]{1,0:T(8,128)S(1)} fusion(bf16[512,512]{0,1:T(8,128)(2,1)} %all_gather.23, bf16[512,1024]{1,0:T(8,128)(2,1)S(1)} %bitcast.35, f32[1024]{0:T(1024)S(1)} %dynamic-slice-done, f32[1024]{0:T(1024)S(1)} %dynamic-slice_multiply_fusion), kind=kOutput, calls=%fused_computation | convolution fusion | flops 537919488 | bytes 3678208 | tf_op jit(solution)/shard_map/dot_general | solution.py:39
  59.9 2.8 fusion.165
  63.1 9.4 %all_gather.21 = f32[128,128]{1,0:T(8,128)S(1)} all-gather(f32[16,128]{1,0:T(8,128)S(1)} %broadcast_multiply_fusion), channel_id=1, replica_groups=mesh['doc'=4,'feat'=8] {'feat'}, dimensions={0}, use_global_device_ids=true | all-gather | bytes 73728 | tf_op jit(solution)/shard_map/all_gather | solution.py:65
  72.5 14.2 %reduce-scatter.7.cloned.1.call-done = f32[1,128,128]{2,1,0:T(8,128)} async-done(((f32[4,128,128]{2,1,0:T(8,128)}), f32[1,128,128]{2,1,0:T(8,128)}) %reduce-scatter.7.cloned.1.call-update) | async-done | bytes 65552 | tf_op jit(solution)/shard_map/reduce_scatter | solution.py:43
  88.5 11.7 %cholesky.18 = f32[128,128]{1,0:T(8,128)S(1)} custom-call(f32[128,128]{1,0:T(8,128)S(1)} %fusion.33), custom_call_target="Cholesky" | custom-call | tf_op jit(solution)/shard_map/jit(cholesky)/cholesky | solution.py:45
  101.6 9.8 %custom-call.6 = f32[1,128,128]{1,2,0:T(8,128)S(1)} custom-call(f32[1,128,128]{2,1,0:T(8,128)S(1)} %fusion.30), custom_call_target="InvertDiagBlocksLowerTriangular" | custom-call | tf_op jit(solution)/shard_map/triangular_solve | solution.py:46
  113.3 4.4 %collective-permute-done = f32[128,128]{1,0:T(8,128)S(1)} collective-permute-done((f32[128,128]{1,0:T(8,128)S(1)}, f32[128,128]{1,0:T(8,128)S(1)}, u32[]{:S(2)}, u32[]{:S(2)}) %collective-permute-start) | collective-permute-done | bytes 65568 | tf_op jit(solution)/shard_map/ppermute | solution.py:75
  119.2 5.6 %collective-permute-done.1 = f32[256,128]{1,0:T(8,128)S(1)} collective-permute-done((f32[256,128]{1,0:T(8,128)S(1)}, f32[256,128]{1,0:T(8,128)S(1)}, u32[]{:S(2)}, u32[]{:S(2)}) %collective-permute-start.1) | collective-permute-done | bytes 131104 | tf_op jit(solution)/shard_map/ppermute | solution.py:75
  124.8 4.1 %multiply_reduce_fusion.1 = (f32[]{:T(128)}, f32[]{:T(128)}, f32[1024,128]{1,0:T(8,128)S(1)}) fusion(f32[512,1024]{1,0:T(8,128)S(1)} %cosine_multiply_fusion, f32[256,128]{1,0:T(8,128)S(1)} %collective-permute-done.1, f32[256,128]{1,0:T(8,128)S(1)} %maximum_select_fusion.6, pred[]{:T(512)S(6)} %eq.13), kind=kOutput, calls=%fused_computation.13 | convolution fusion | flops 807075840 | bytes 2883593 | tf_op jit(solution)/shard_map/dot_general | solution.py:81
  128.9 2.5 fusion.6
  131.5 20.5 %reduce-scatter.9.cloned.1.call-done = f32[16,128]{1,0:T(8,128)} async-done(((f32[128,128]{1,0:T(8,128)}), f32[16,128]{1,0:T(8,128)}) %reduce-scatter.9.cloned.1.call-update) | async-done | bytes 8208 | tf_op jit(solution)/shard_map/reduce_scatter | solution.py:71
  157.9 39.3 %all-reduce.1 = (f32[]{:T(128)}, f32[]{:T(128)}) all-reduce(f32[]{:T(128)S(6)} %add.203, f32[]{:T(128)S(6)} %add.205), channel_id=1, replica_groups=mesh['doc'=4,'feat'=8] {'doc','feat'}, use_global_device_ids=true, to_apply=%region_7.8 | all-reduce | flops 2 | bytes 16 | tf_op jit(solution)/shard_map/psum | solution.py:102
  199.2 10.2 %all_gather.24 = f32[128,128]{1,0:T(8,128)S(1)} all-gather(f32[16,128]{1,0:T(8,128)S(1)} %subtract_multiply_fusion.2), channel_id=1, replica_groups=mesh['doc'=4,'feat'=8] {'feat'}, dimensions={0}, use_global_device_ids=true | all-gather | bytes 73728 | tf_op jit(solution)/shard_map/all_gather | solution.py:65
  213.2 2.9 collective-permute-done.2
  216.1 2.3 collective-permute-start.3
  218.8 6.1 %collective-permute-done.3 = f32[256,128]{1,0:T(8,128)} collective-permute-done((f32[256,128]{1,0:T(8,128)S(1)}, f32[256,128]{1,0:T(8,128)}, u32[]{:S(2)}, u32[]{:S(2)}) %collective-permute-start.3) | collective-permute-done | bytes 131104 | tf_op jit(solution)/shard_map/ppermute | solution.py:75
  224.9 5.2 %multiply_reduce_fusion = (f32[]{:T(128)}, f32[]{:T(128)}, f32[1024,128]{1,0:T(8,128)S(1)}) fusion(f32[1024,128]{1,0:T(8,128)S(1)} %get-tuple-element.24, f32[]{:T(128)S(6)} %neg.66, f32[]{:T(128)S(6)} %div.199, f32[]{:T(128)S(6)} %pow.6, f32[512,1024]{1,0:T(8,128)S(1)} %cosine_multiply_fusion, f32[256,128]{1,0:T(8,128)} %collective-permute-done.3, ...), kind=kOutput, calls=%fused_computation.11 | convolution fusion | flops 808386560 | bytes 3407893 | tf_op jit(solution)/shard_map/dot_general | solution.py:81
  230.1 2.5 fusion.160
  232.8 17.6 %reduce-scatter.13.cloned.1.call-done = f32[16,128]{1,0:T(8,128)} async-done(((f32[128,128]{1,0:T(8,128)}), f32[16,128]{1,0:T(8,128)}) %reduce-scatter.13.cloned.1.call-update) | async-done | bytes 8208 | tf_op jit(solution)/shard_map/reduce_scatter | solution.py:71
  255.0 39.3 %all-reduce = (f32[]{:T(128)}, f32[]{:T(128)}) all-reduce(f32[]{:T(128)S(6)} %add.219, f32[]{:T(128)S(6)} %add.221), channel_id=1, replica_groups=mesh['doc'=4,'feat'=8] {'doc','feat'}, use_global_device_ids=true, to_apply=%region_16.17 | all-reduce | flops 2 | bytes 16 | tf_op jit(solution)/shard_map/psum | solution.py:102
  296.3 10.2 %all_gather.25 = f32[128,128]{1,0:T(8,128)S(1)} all-gather(f32[16,128]{1,0:T(8,128)S(1)} %subtract_multiply_fusion.1), channel_id=1, replica_groups=mesh['doc'=4,'feat'=8] {'feat'}, dimensions={0}, use_global_device_ids=true | all-gather | bytes 73728 | tf_op jit(solution)/shard_map/all_gather | solution.py:65
  309.7 2.9 collective-permute-done.4
  312.6 2.3 collective-permute-start.5
  315.2 6.2 %collective-permute-done.5 = f32[256,128]{1,0:T(8,128)S(1)} collective-permute-done((f32[256,128]{1,0:T(8,128)S(1)}, f32[256,128]{1,0:T(8,128)S(1)}, u32[]{:S(2)}, u32[]{:S(2)}) %collective-permute-start.5) | collective-permute-done | bytes 131104 | tf_op jit(solution)/shard_map/ppermute | solution.py:75
  321.3 4.2 %subtract_multiply_fusion = f32[1024,128]{1,0:T(8,128)} fusion(f32[512,1024]{1,0:T(8,128)S(1)} %cosine_multiply_fusion, f32[256,128]{1,0:T(8,128)S(1)} %collective-permute-done.5, f32[256,128]{1,0:T(8,128)S(1)} %maximum_select_fusion.8, f32[]{:T(128)S(6)} %neg.70, f32[]{:T(128)S(6)} %div.220, pred[]{:T(512)S(6)} %eq.13, f32[]{:T(128)S(6)} %neg.66, ...), kind=kOutput, calls=%fused_computation.10 | convolution fusion | flops 807337984 | bytes 3932177 | tf_op jit(solution)/shard_map/dot_general | solution.py:81
  325.7 21.2 %reduce-scatter.17.cloned.1.call-done = f32[16,128]{1,0:T(8,128)} async-done(((f32[128,128]{1,0:T(8,128)}), f32[16,128]{1,0:T(8,128)}) %reduce-scatter.17.cloned.1.call-update) | async-done | bytes 8208 | tf_op jit(solution)/shard_map/reduce_scatter | solution.py:71
  347.8 9.2 %all_gather.26 = f32[128,128]{1,0:T(8,128)S(1)} all-gather(f32[16,128]{1,0:T(8,128)S(1)} %fusion.83), channel_id=1, replica_groups=mesh['doc'=4,'feat'=8] {'feat'}, dimensions={0}, use_global_device_ids=true | all-gather | bytes 73728 | tf_op jit(solution)/shard_map/all_gather | solution.py:112
  357.0 37.8 %all-gather.2.cloned.1.call-done = f32[4096,128]{1,0:T(8,128)} async-done(((f32[1024,128]{1,0:T(8,128)}), f32[4096,128]{1,0:T(8,128)}) %all-gather.2.cloned.1.call-update) | async-done | bytes 2097168 | tf_op jit(solution)/shard_map/all_gather | solution.py:113
  395.4 3.0 copy.16
  (81 shorter events, 25.2 us)
Async XLA Ops:
  7.2 8.6 %copy-start.6 = (bf16[128,64]{0,1:T(8,128)(2,1)S(1)}, bf16[128,64]{0,1:T(8,128)(2,1)}, u32[]{:S(2)}) copy-start(bf16[128,64]{0,1:T(8,128)(2,1)} %param.6) | copy-start | bytes 49156
  9.4 41.6 %all-to-all-start = ((bf16[128,4,1024]{0,2,1:T(8,128)(2,1)}), bf16[128,4,1024]{0,2,1:T(8,128)(2,1)S(1)}, u32[]{:S(2)}, u32[]{:S(2)}) async-start(bf16[128,4,1024]{0,2,1:T(8,128)(2,1)} %bitcast), calls=%async_computation | async-start | bytes 2097152 | tf_op jit(solution)/shard_map/all_to_all | solution.py:36
  15.8 70.9 %reduce-scatter.7.cloned.1.call-start = ((), (), s32[]{:S(2)}) async-start(), calls=%async_computation.7 | async-start | bytes 327680 | tf_op jit(solution)/shard_map/reduce_scatter | solution.py:43
  15.8 35.8 %dynamic-slice-start = ((f32[4096]{0:T(1024)}, s32[]{:T(128)}), f32[1024]{0:T(1024)S(1)}, s32[]{:S(2)}) async-start(f32[4096]{0:T(1024)} %param.8, s32[]{:T(128)} %select_n.50), calls=%async_computation.14 | async-start | bytes 8704 | tf_op jit(solution)/shard_map/dynamic_slice | solution.py:37
  59.9 2.9 copy-start.13
  59.9 2.9 copy-start.10
  62.7 89.3 %reduce-scatter.9.cloned.1.call-start = ((), (), s32[]{:S(2)}) async-start(), calls=%async_computation.8 | async-start | bytes 73728 | tf_op jit(solution)/shard_map/reduce_scatter | solution.py:71
  62.9 89.2 %copy-start.7 = (s32[16]{0:T(128)}, s32[16]{0:T(128)S(1)}, u32[]{:S(2)}) copy-start(s32[16]{0:T(128)S(1)} %dynamic-slice) | copy-start | bytes 196
  113.3 4.4 %collective-permute-start = (f32[128,128]{1,0:T(8,128)S(1)}, f32[128,128]{1,0:T(8,128)S(1)}, u32[]{:S(2)}, u32[]{:S(2)}) collective-permute-start(f32[128,128]{1,0:T(8,128)S(1)} %get-tuple-element.23), channel_id=1, source_target_pairs={{0,8},{8,0},{16,24},{24,16},{1,9},{9,1},{17,25},{25,17},{2,10},{10... | collective-permute-start | bytes 196616 | tf_op jit(solution)/shard_map/ppermute | solution.py:75
  117.8 7.0 %collective-permute-start.1 = (f32[256,128]{1,0:T(8,128)S(1)}, f32[256,128]{1,0:T(8,128)S(1)}, u32[]{:S(2)}, u32[]{:S(2)}) collective-permute-start(f32[256,128]{1,0:T(8,128)S(1)} %maximum_select_fusion.6), channel_id=1, source_target_pairs={{0,16},{8,24},{16,0},{24,8},{1,17},{9,25},{17,1},{25,9},{2,18},{10... | collective-permute-start | bytes 393224 | tf_op jit(solution)/shard_map/ppermute | solution.py:75
  118.9 90.5 %reduce-scatter.11.cloned.1.call-start = ((), (), s32[]{:S(2)}) async-start(), calls=%async_computation.9 | async-start | bytes 327680 | tf_op jit(solution)/shard_map/reduce_scatter | solution.py:105
  128.9 80.5 %copy-start = (f32[128,128]{1,0:T(8,128)S(1)}, f32[128,128]{1,0:T(8,128)}, u32[]{:S(2)}) copy-start(f32[128,128]{1,0:T(8,128)} %get-tuple-element.20) | copy-start | bytes 196612
  131.4 119.0 %reduce-scatter.13.cloned.1.call-start = ((), (), s32[]{:S(2)}) async-start(), calls=%async_computation.10 | async-start | bytes 73728 | tf_op jit(solution)/shard_map/reduce_scatter | solution.py:71
  211.7 4.4 %collective-permute-start.2 = (f32[128,128]{1,0:T(8,128)S(1)}, f32[128,128]{1,0:T(8,128)S(1)}, u32[]{:S(2)}, u32[]{:S(2)}) collective-permute-start(f32[128,128]{1,0:T(8,128)S(1)} %get-tuple-element.25), channel_id=1, source_target_pairs={{0,8},{8,0},{16,24},{24,16},{1,9},{9,1},{17,25},{25,17},{2,10},{10... | collective-permute-start | bytes 196616 | tf_op jit(solution)/shard_map/ppermute | solution.py:75
  216.1 8.8 %collective-permute-start.3 = (f32[256,128]{1,0:T(8,128)S(1)}, f32[256,128]{1,0:T(8,128)}, u32[]{:S(2)}, u32[]{:S(2)}) collective-permute-start(f32[256,128]{1,0:T(8,128)S(1)} %maximum_select_fusion.7), channel_id=1, source_target_pairs={{0,16},{8,24},{16,0},{24,8},{1,17},{9,25},{17,1},{25,9},{2,18},{10... | collective-permute-start | bytes 393224 | tf_op jit(solution)/shard_map/ppermute | solution.py:75
  218.5 88.0 %reduce-scatter.15.cloned.1.call-start = ((), (), s32[]{:S(2)}) async-start(), calls=%async_computation.11 | async-start | bytes 327680 | tf_op jit(solution)/shard_map/reduce_scatter | solution.py:105
  230.1 2.6 copy-start.11
  230.1 20.3 %copy-start.8 = (s32[16]{0:T(128)S(1)}, s32[16]{0:T(128)}, u32[]{:S(2)}) copy-start(s32[16]{0:T(128)} %copy-done.7) | copy-start | bytes 196
  230.1 76.5 %copy-start.1 = (f32[128,128]{1,0:T(8,128)S(1)}, f32[128,128]{1,0:T(8,128)}, u32[]{:S(2)}) copy-start(f32[128,128]{1,0:T(8,128)} %reduce-scatter.11.cloned.1.call-done) | copy-start | bytes 196612
  230.1 76.5 %copy-start.2 = (f32[128,128]{1,0:T(8,128)S(1)}, f32[128,128]{1,0:T(8,128)}, u32[]{:S(2)}) copy-start(f32[128,128]{1,0:T(8,128)} %get-tuple-element.22) | copy-start | bytes 196612
  232.6 114.3 %reduce-scatter.17.cloned.1.call-start = ((), (), s32[]{:S(2)}) async-start(), calls=%async_computation.12 | async-start | bytes 73728 | tf_op jit(solution)/shard_map/reduce_scatter | solution.py:71
  251.9 43.7 %copy-start.4 = (f32[16,128]{1,0:T(8,128)}, f32[16,128]{1,0:T(8,128)S(1)}, u32[]{:S(2)}) copy-start(f32[16,128]{1,0:T(8,128)S(1)} %get-tuple-element.12) | copy-start | bytes 24580
  308.2 4.4 %collective-permute-start.4 = (f32[128,128]{1,0:T(8,128)S(1)}, f32[128,128]{1,0:T(8,128)S(1)}, u32[]{:S(2)}, u32[]{:S(2)}) collective-permute-start(f32[128,128]{1,0:T(8,128)S(1)} %get-tuple-element.28), channel_id=1, source_target_pairs={{0,8},{8,0},{16,24},{24,16},{1,9},{9,1},{17,25},{25,17},{2,10},{10... | collective-permute-start | bytes 196616 | tf_op jit(solution)/shard_map/ppermute | solution.py:75
  312.6 8.7 %collective-permute-start.5 = (f32[256,128]{1,0:T(8,128)S(1)}, f32[256,128]{1,0:T(8,128)S(1)}, u32[]{:S(2)}, u32[]{:S(2)}) collective-permute-start(f32[256,128]{1,0:T(8,128)S(1)} %maximum_select_fusion.8), channel_id=1, source_target_pairs={{0,16},{8,24},{16,0},{24,8},{1,17},{9,25},{17,1},{25,9},{2,18},{10... | collective-permute-start | bytes 393224 | tf_op jit(solution)/shard_map/ppermute | solution.py:75
  315.1 10.5 %copy-start.12 = (f32[128]{0:T(128)S(1)}, f32[128]{0:T(128)}, u32[]{:S(2)}) copy-start(f32[128]{0:T(128)} %param.10) | copy-start | bytes 1540
  315.1 31.9 %copy-start.3 = (f32[16,128]{1,0:T(8,128)S(1)}, f32[16,128]{1,0:T(8,128)}, u32[]{:S(2)}) copy-start(f32[16,128]{1,0:T(8,128)} %reduce-scatter.13.cloned.1.call-done) | copy-start | bytes 24580
  315.1 31.9 %copy-start.5 = (f32[16,128]{1,0:T(8,128)S(1)}, f32[16,128]{1,0:T(8,128)}, u32[]{:S(2)}) copy-start(f32[16,128]{1,0:T(8,128)} %copy-done.4) | copy-start | bytes 24580
  315.1 31.9 %copy-start.9 = (s32[16]{0:T(128)S(1)}, s32[16]{0:T(128)}, u32[]{:S(2)}) copy-start(s32[16]{0:T(128)} %copy-done.7) | copy-start | bytes 196
  315.1 79.7 %all-gather.2.cloned.1.call-start = ((), (), s32[]{:S(2)}) async-start(), calls=%async_computation.13 | async-start | bytes 2621440 | tf_op jit(solution)/shard_map/all_gather | solution.py:113
Sparse Core Ops, SparseCore 0:
  62.8 23.8 reduce-scatter.6
  119.0 32.9 reduce-scatter.8
  154.9 19.9 reduce-scatter.10
  218.6 31.7 reduce-scatter.12
  253.1 19.9 reduce-scatter.14
  315.2 31.7 reduce-scatter.16
  349.1 45.6 all-gather.1
